TPU v7x, 32 devices: a whole 2x2x4 slice. The times are simulated.
32 devices in a mesh: frame: 4 (over x, core), cam: 8 (over z, y).
Axes of the slice: x: 2, y: 2, z: 4, core: 2. Of those that a mesh axis runs over, the one named last changes fastest.
Arguments:
- view_maps: bfloat16 [8, 88, 2, 32, 256], P('frame', 'cam'), may hold values from -6 to 6
- conv_weight: bfloat16 [9, 256, 256], replicated, may hold values from -0.125 to 0.125
- join_weight: bfloat16 [16384, 256], P('cam'), may hold values from -0.1875 to 0.1875
- valid_cams: int32 [8, 88], P('frame'), may hold values from 0 to 1, as said below
- latent_grad: bfloat16 [8, 256], P('frame'), may hold values from -6 to 6
Outputs:
- latent: float32 [8, 256], P('frame')
- conv_grad: float32 [9, 256, 256], replicated
- join_grad: float32 [16384, 256], P(('cam', 'frame'))
Inputs may be any that keep to these rules, and one draw needn't show every extreme that they name: `valid_cams`: every frame has at least one usable camera; the last 6 cameras are padding and never usable.
All inputs are finite; a program needn't handle non-finite values.
Results may differ from a plain program's by a relative error of at most 0.007.
Values may be sent and summed in bfloat16 or wider, within the bound.
A program may use at most 64 MiB of HBM per device.

v0:
```python
import jax
import jax.numpy as jnp
from jax import lax
from jax.sharding import PartitionSpec as P


def make_shifts(maps, rows_n, cols_n, chans):
    padded = jnp.pad(maps, ((0, 0), (0, 0), (1, 1), (1, 1), (0, 0)))
    return [
        padded[:, :, dy : dy + rows_n, dx : dx + cols_n, :].reshape(-1, chans)
        for dy in range(3)
        for dx in range(3)
    ]


def on_device(view_maps, conv_weight, join_weight, valid_cams, latent_grad):
    frames_here, cams_here, rows_n, cols_n, chans = view_maps.shape
    feat_len = rows_n * cols_n * chans
    shifted = make_shifts(view_maps, rows_n, cols_n, chans)
    preact = jnp.zeros((frames_here * cams_here * rows_n * cols_n, chans), jnp.float32)
    for k in range(9):
        preact = preact + jnp.dot(shifted[k], conv_weight[k], preferred_element_type=jnp.float32)
    sigma = jax.nn.sigmoid(preact)
    features = (preact * sigma).astype(jnp.bfloat16)
    features = features.reshape(frames_here, cams_here, feat_len)
    slopes = (sigma * (1.0 + preact * (1.0 - sigma))).reshape(frames_here, cams_here, feat_len)
    cam_count = jnp.sum(valid_cams.astype(jnp.float32), axis=1)
    local_valid = lax.dynamic_slice_in_dim(
        valid_cams, lax.axis_index("cam") * cams_here, cams_here, 1
    )
    mask_f = local_valid.astype(jnp.float32)
    mask_b = local_valid.astype(jnp.bfloat16)
    share_len = feat_len // lax.axis_size("cam")
    pooled = lax.psum_scatter(
        jnp.einsum("fc,fcp->pf", mask_b, features, preferred_element_type=jnp.float32),
        "cam",
        scatter_dimension=0,
        tiled=True,
    )
    joined = (pooled.T / cam_count[:, None]).astype(jnp.bfloat16)
    partial_latent = jnp.dot(joined, join_weight, preferred_element_type=jnp.float32)
    latent = lax.psum(partial_latent, "cam")
    joined_grad = jnp.einsum(
        "fl,sl->fs", latent_grad, join_weight, preferred_element_type=jnp.float32
    ).astype(jnp.bfloat16)
    weighting = mask_f / cam_count[:, None]
    scaled = (
        lax.all_gather(joined_grad, "cam", axis=1, tiled=True).astype(jnp.float32)[:, None, :]
        * weighting[:, :, None]
        * slopes
    )
    pre_grad = scaled.astype(jnp.bfloat16)
    pre_grad = pre_grad.reshape(-1, chans)
    taps = jnp.stack(
        [
            lax.dot_general(
                shifted[k], pre_grad, (((0,), (0,)), ((), ())), preferred_element_type=jnp.float32
            )
            for k in range(9)
        ]
    )
    sub_len = share_len // lax.axis_size("frame")
    all_joined, all_cotangent = (
        lax.all_gather(joined, "frame", axis=0, tiled=True),
        lax.all_gather(latent_grad, "frame", axis=0, tiled=True),
    )
    own_rows = lax.dynamic_slice_in_dim(all_joined, lax.axis_index("frame") * sub_len, sub_len, 1)
    join_grad = lax.dot_general(
        own_rows, all_cotangent, (((0,), (0,)), ((), ())), preferred_element_type=jnp.float32
    )
    conv_grad = lax.psum(taps, ("frame", "cam"))
    return (latent, conv_grad, join_grad)


def solution(mesh):
    in_specs = (
        P("frame", "cam", None, None, None),
        P(),
        P("cam", None),
        P("frame", None),
        P("frame", None),
    )
    out_specs = (P("frame", None), P(), P(("cam", "frame"), None))
    return jax.shard_map(
        on_device, mesh=mesh, in_specs=in_specs, out_specs=out_specs, check_vma=False
    )
```

profile of v0, /device:TPU:0, one launch (start us, length us, event | category | flops | bytes accessed | tf_op | source)
XLA Modules:
  0.0 305.6 jit_solution(8454710060224463295)
XLA Ops:
  8.1 4.9 %pad_slice_fusion = (bf16[2,11,2,32,256]{4,3,2,1,0:T(8,128)(2,1)}, bf16[2,11,2,32,256]{4,3,2,1,0:T(8,128)(2,1)}, bf16[2,11,2,32,256]{4,3,2,1,0:T(8,128)(2,1)}, b...) fusion(bf16[2,11,2,32,256]{4,3,2,1,0:T(8,128)(2,1)} %param.5), kind=kLoop, calls=%fused_computation | loop fusion | bytes 6488064 | tf_op jit(solution)/shard_map/slice | solution.py:10
  13.0 0.1 convert_reduce_fusion
  13.3 0.4 convolution_convert_fusion
  13.7 32.4 %all_gather.9 = bf16[2,16384]{1,0:T(2,128)(2,1)S(1)} all-gather(bf16[2,2048]{1,0:T(2,128)(2,1)S(1)} %convolution_convert_fusion), channel_id=1, replica_groups=mesh['frame'=4,'cam'=8] {'cam'}, dimensions={1}, use_global_device_ids=true | all-gather | bytes 73728 | tf_op jit(solution)/shard_map/all_gather | solution.py:48
  46.1 0.2 broadcast_multiply_fusion
  46.3 1.4 mul.41
  47.7 1.6 fusion.17
  49.4 0.1 copy-done.15
  49.5 0.3 convolution_add_fusion.7
  49.8 0.8 copy-done.9
  50.6 0.3 convolution_add_fusion.6
  50.9 0.8 copy-done.7
  51.7 0.3 convolution_add_fusion.5
  52.1 0.8 copy-done.1
  52.8 0.3 convolution_add_fusion.4
  53.2 0.8 copy-done.5
  53.9 0.4 convolution_add_fusion.3
  54.3 0.8 copy-done.3
  55.0 0.4 convolution_add_fusion.2
  55.4 0.8 copy-done.2
  56.2 0.4 convolution_add_fusion.1
  56.5 1.0 copy-done.14
  57.5 0.2 copy-done.16
  57.7 1.9 multiply_convert_fusion
  59.6 1.6 reshape.53
  61.2 0.3 fusion.30
  61.5 0.1 copy.19
  61.6 4.9 %copy.14 = f32[16384,2]{1,0:T(8,128)} copy(f32[16384,2]{0,1:T(2,128)S(1)} %bitcast.140) | data formatting | bytes 262144
  66.6 1.0 copy-done.13
  67.6 2.3 fusion.8
  69.9 1.1 fusion.7
  71.0 1.1 fusion.6
  72.2 1.1 fusion.5
  73.3 1.1 fusion.4
  74.4 1.1 fusion.3
  75.5 1.1 fusion.2
  76.6 1.1 fusion.1
  77.7 1.1 fusion
  78.9 5.1 %all-gather.1 = bf16[4,2,256]{2,1,0:T(2,128)(2,1)S(1)} all-gather(bf16[1,2,256]{2,1,0:T(2,128)(2,1)S(1)} %bitcast.141), channel_id=1, replica_groups=mesh['frame'=4,'cam'=8] {'frame'}, dimensions={0}, use_global_device_ids=true | all-gather | bytes 5120 | tf_op jit(solution)/shard_map/all_gather | solution.py:65
  84.0 142.1 %reduce-scatter.4.cloned.1.call-done = f32[2048,2]{1,0:T(8,128)} async-done(((f32[16384,2]{1,0:T(8,128)}), f32[2048,2]{1,0:T(8,128)}) %reduce-scatter.4.cloned.1.call-update) | async-done | bytes 16400
  226.0 1.6 copy.15
  227.6 0.1 fusion.68
  227.7 5.2 %all-gather = bf16[4,2,2048]{2,1,0:T(2,128)(2,1)S(1)} all-gather(bf16[1,2,2048]{2,1,0:T(2,128)(2,1)S(1)} %fusion.68), channel_id=1, replica_groups=mesh['frame'=4,'cam'=8] {'frame'}, dimensions={0}, use_global_device_ids=true | all-gather | bytes 40960 | tf_op jit(solution)/shard_map/all_gather | solution.py:64
  232.9 0.3 fusion.34
  233.2 20.2 %psum.14 = f32[2,256]{1,0:T(2,128)} all-reduce(f32[2,256]{1,0:T(2,128)S(1)} %fusion.34), channel_id=1, replica_groups=mesh['frame'=4,'cam'=8] {'cam'}, use_global_device_ids=true, to_apply=%region_2.3 | all-reduce | flops 512 | bytes 4096 | tf_op jit(solution)/shard_map/psum | solution.py:42
  253.4 1.1 fusion.28
  254.4 40.5 %all-reduce.3.cloned.1.call-done = f32[9,256,256]{2,1,0:T(8,128)} async-done(((f32[9,256,256]{2,1,0:T(8,128)}), f32[9,256,256]{2,1,0:T(8,128)}) %all-reduce.3.cloned.1.call-update) | async-done | bytes 2359312 | tf_op jit(solution)/shard_map/psum | solution.py:71
  294.9 3.2 %copy.29 = f32[9,256,256]{2,1,0:T(8,128)} copy(f32[9,256,256]{2,1,0:T(8,128)} %all-reduce.3.cloned.1.call-done) | data formatting | bytes 4718592
  (41 shorter events, 0.4 us)
Async XLA Ops:
  8.0 5.3 %copy-start = (bf16[2048,256]{1,0:T(8,128)(2,1)S(1)}, bf16[2048,256]{1,0:T(8,128)(2,1)}, u32[]{:S(2)}) copy-start(bf16[2048,256]{1,0:T(8,128)(2,1)} %param.7) | copy-start | bytes 3145732
  8.0 218.0 %reduce-scatter.4.cloned.1.call-start = ((), (), s32[]{:S(2)}) async-start(), calls=%async_computation.2 | async-start | bytes 9437184
  8.1 5.0 %copy-start.20 = (s32[2,88]{1,0:T(2,128)S(1)}, s32[2,88]{1,0:T(2,128)}, u32[]{:S(2)}) copy-start(s32[2,88]{1,0:T(2,128)} %param.8) | copy-start | bytes 2116
  8.1 5.2 %copy-start.19 = (bf16[2,256]{1,0:T(2,128)(2,1)S(1)}, bf16[2,256]{1,0:T(2,128)(2,1)}, u32[]{:S(2)}) copy-start(bf16[2,256]{1,0:T(2,128)(2,1)} %param.9) | copy-start | bytes 3076
  47.7 1.6 copy-start.11
  47.7 1.7 copy-start.15
  49.5 1.1 copy-start.9
  50.6 1.1 copy-start.7
  51.7 1.1 copy-start.1
  52.8 1.1 copy-start.5
  53.9 1.1 copy-start.3
  55.0 1.1 copy-start.2
  56.1 1.4 copy-start.14
  56.1 1.5 copy-start.16
  66.5 1.1 copy-start.13
  66.5 228.4 %all-reduce.3.cloned.1.call-start = ((), (), s32[]{:S(2)}) async-start(), calls=%async_computation.1 | async-start | bytes 4718592 | tf_op jit(solution)/shard_map/psum | solution.py:71
  66.6 3.3 %copy-start.12 = (bf16[2,11,2,32,256]{4,3,2,1,0:T(8,128)(2,1)S(1)}, bf16[2,11,2,32,256]{4,3,2,1,0:T(8,128)(2,1)}, u32[]{:S(2)}) copy-start(bf16[2,11,2,32,256]{4,3,2,1,0:T(8,128)(2,1)} %get-tuple-element.6) | copy-start | bytes 2162692
  66.6 3.3 %copy-start.18 = (bf16[1408,256]{1,0:T(8,128)(2,1)S(1)}, bf16[1408,256]{1,0:T(8,128)(2,1)}, u32[]{:S(2)}) copy-start(bf16[1408,256]{1,0:T(8,128)(2,1)} %get-tuple-element.3) | copy-start | bytes 2162692
  67.6 3.4 %copy-start.10 = (bf16[2,11,2,32,256]{4,3,2,1,0:T(8,128)(2,1)S(1)}, bf16[2,11,2,32,256]{4,3,2,1,0:T(8,128)(2,1)}, u32[]{:S(2)}) copy-start(bf16[2,11,2,32,256]{4,3,2,1,0:T(8,128)(2,1)} %get-tuple-element.7) | copy-start | bytes 2162692
  69.9 2.2 copy-start.8
  72.2 2.2 copy-start.6
  73.3 2.2 copy-start.4
  75.5 2.2 copy-start.17
Sparse Core Ops, SparseCore 0:
  66.7 159.3 reduce-scatter.3
Sparse Core Ops, SparseCore 1:
  79.0 215.9 all-reduce.2
where the time goes:
time: 306 us
  waiting for transfers between devices  183 us (60%)
  blocking collectives  62.8 us (21%)
  local copies, waits for them, and re-layouts  24.7 us (8%)
  matrix products  19.2 us (6%)
  between operations  15.6 us (5%)
    unnamed x3, waiting for transfers between devices  142 us
    psum x1, waiting for transfers between devices, on_device(): conv_grad = lax.psum(taps, ('frame', 'cam'))  40.5 us
    all_gather x1, blocking collectives, on_device(): lax.all_gather(joined_grad, 'cam', axis=1, tiled=True).astype(jnp.float32)  32.4 us
    psum x1, blocking collectives, on_device(): latent = lax.psum(partial_latent, 'cam')  20.2 us
    unnamed x47, local copies, waits for them, and re-layouts  16.6 us
    dot_general x9, matrix products, on_device(): lax.dot_general(shifted[k], pre_grad, (((0,), (0,)), ((), ())), preferred...  11.2 us
  transfers between devices with their start and end apart: 2, of which 2 were waited for; matrix products, arithmetic and copies ran while one was open for 5% of the time, Pallas kernels for 0%

commit v1 on v0

--- a/solution.py
+++ b/solution.py
@@ -2,6 +2,18 @@
 import jax.numpy as jnp
 from jax import lax
 from jax.sharding import PartitionSpec as P
+
+
+def collect(array, axis, dim):
+    ways, here, lap = (lax.axis_size(axis), lax.axis_index(axis), array.shape[dim])
+    line, have = (array, 1)
+    while have < ways:
+        line = jnp.concatenate(
+            [line, lax.ppermute(line, axis, [(d, (d - have) % ways) for d in range(ways)])],
+            axis=dim,
+        )
+        have = 2 * have
+    return jnp.roll(line, here * lap, axis=dim)
 
 
 def make_shifts(maps, rows_n, cols_n, chans):
@@ -45,7 +57,7 @@
     ).astype(jnp.bfloat16)
     weighting = mask_f / cam_count[:, None]
     scaled = (
-        lax.all_gather(joined_grad, "cam", axis=1, tiled=True).astype(jnp.float32)[:, None, :]
+        collect(joined_grad, "cam", 1).astype(jnp.float32)[:, None, :]
         * weighting[:, :, None]
         * slopes
     )

time: 306 us -> 292 us (0.954)
  blocking collectives: 62.8 us -> 30.4 us
  waiting for transfers between devices: 183 us -> 198 us
  starting transfers between devices: 0.08 us -> 6.67 us
  matrix products: 19.2 us -> 13 us
  other arithmetic: 0.61 us -> 3.8 us
    all_gather x1 -> x0, blocking collectives: 32.4 us -> none  [on_device(): lax.all_gather(joined_grad, 'cam', axis=1, tiled=True).astype(jnp.float32)]
    ppermute x0 -> x3, waiting for transfers between devices: none -> 8.07 us  [collect(): lax.ppermute(line, axis, [(d, (d - have) % ways) for d in range(ways)])]
    unnamed x3, waiting for transfers between devices: 142 us -> 150 us
    dot_general x9, matrix products: 11.2 us -> 4.42 us  [on_device(): lax.dot_general(shifted[k], pre_grad, (((0,), (0,)), ((), ())), preferred...]
    ppermute x0 -> x3, starting transfers between devices: none -> 6.59 us  [collect(): lax.ppermute(line, axis, [(d, (d - have) % ways) for d in range(ways)])]
    unnamed x47 -> x55, local copies, waits for them, and re-layouts: 16.6 us -> 18.9 us
  transfers between devices with their start and end apart: 2 -> 5, of which waited for: 2 -> 4; matrix products, arithmetic and copies ran while one was open for 5% -> 5% of each run, Pallas kernels for 0% -> 0%
where the time goes in v1:
time: 292 us; the launch traced here: 291 us
  waiting for transfers between devices  198 us (68%)
  blocking collectives  30.4 us (10%)
  local copies, waits for them, and re-layouts  23.4 us (8%)
  between operations  15.8 us (5%)
  matrix products  13 us (4%)
  starting transfers between devices  6.67 us (2%)
  other arithmetic  3.8 us (1%)
    unnamed x3, waiting for transfers between devices  150 us
    psum x1, waiting for transfers between devices, on_device(): conv_grad = lax.psum(taps, ('frame', 'cam'))  40.5 us
    psum x1, blocking collectives, on_device(): latent = lax.psum(partial_latent, 'cam')  20.2 us
    unnamed x55, local copies, waits for them, and re-layouts  18.9 us
    ppermute x3, waiting for transfers between devices, collect(): lax.ppermute(line, axis, [(d, (d - have) % ways) for d in range(ways)])  8.07 us
    ppermute x3, starting transfers between devices, collect(): lax.ppermute(line, axis, [(d, (d - have) % ways) for d in range(ways)])  6.59 us
    dot_general x9, matrix products, on_device(): jnp.dot(shifted[k], conv_weight[k], preferred_element_type=jnp.float32)  5.93 us
  transfers between devices with their start and end apart: 5, of which 4 were waited for; matrix products, arithmetic and copies ran while one was open for 5% of the time, Pallas kernels for 0%

profile of v1, /device:TPU:0, one launch (start us, length us, event | category | flops | bytes accessed | tf_op | source)
XLA Modules:
  0.0 291.4 jit_solution(17301035568372068742)
XLA Ops:
  8.1 1.2 copy-done
  9.2 1.0 constant_dynamic-update-slice_fusion.7
  10.3 6.0 %collective-permute-start = (bf16[2,2048]{1,0:T(2,128)(2,1)S(1)}, bf16[2,2048]{1,0:T(2,128)(2,1)S(1)}, u32[]{:S(2)}, u32[]{:S(2)}) collective-permute-start(bf16[2,2048]{1,0:T(2,128)(2,1)S(1)} %get-tuple-element.14), channel_id=1, source_target_pairs={{0,7},{1,0},{2,1},{3,2},{4,3},{5,4},{6,5},{7,6},{8,15},{9,8},{10,9... | collective-permute-start | bytes 24584 | tf_op jit(solution)/shard_map/ppermute | solution.py:12
  16.3 0.8 convert_reduce_fusion
  17.1 2.5 pad_slice_fusion
  19.7 2.0 fusion.17
  21.9 0.3 convolution_add_fusion.7
  22.2 0.8 copy-done.13
  23.0 0.3 convolution_add_fusion.6
  23.3 0.8 copy-done.11
  24.1 0.3 convolution_add_fusion.5
  24.5 0.4 convolution_add_fusion.4
  24.8 0.7 copy-done.9
  25.6 0.3 convolution_add_fusion.3
  25.9 0.8 copy-done.7
  26.7 0.3 convolution_add_fusion.2
  27.0 0.3 convolution_add_fusion.1
  27.4 1.5 convolution_add_fusion
  29.0 0.5 collective-permute-start.1
  29.5 3.3 %collective-permute-done.1 = bf16[2,4096]{1,0:T(2,128)(2,1)S(1)} collective-permute-done((bf16[2,4096]{1,0:T(2,128)(2,1)S(1)}, bf16[2,4096]{1,0:T(2,128)(2,1)S(1)}, u32[]{:S(2)}, u32[]{:S(2)}) %collective-permute-start.1) | collective-permute-done | bytes 16416 | tf_op jit(solution)/shard_map/ppermute | solution.py:12
  32.9 4.8 %collective-permute-done.2 = bf16[2,8192]{1,0:T(2,128)(2,1)S(1)} collective-permute-done((bf16[2,8192]{1,0:T(2,128)(2,1)S(1)}, bf16[2,8192]{1,0:T(2,128)(2,1)S(1)}, u32[]{:S(2)}, u32[]{:S(2)}) %collective-permute-start.2) | collective-permute-done | bytes 32800 | tf_op jit(solution)/shard_map/ppermute | solution.py:12
  38.1 1.4 mul.45
  39.5 2.5 multiply_convert_fusion
  42.0 0.4 fusion.8
  42.4 0.7 copy-done.16
  43.1 0.4 fusion.7
  43.5 0.4 fusion.6
  44.0 0.3 copy-done.12
  44.3 0.4 fusion.5
  44.7 0.4 fusion.4
  45.4 0.4 fusion.3
  45.9 0.4 fusion.2
  46.3 0.3 copy-done.6
  46.6 0.4 fusion.1
  47.0 1.4 copy-done.18
  48.4 0.5 reshape.53
  49.3 5.0 %copy.14 = f32[16384,2]{1,0:T(8,128)} copy(f32[16384,2]{0,1:T(2,128)S(1)} %bitcast.138) | data formatting | bytes 262144
  54.3 1.0 copy-done.4
  55.4 1.1 fusion
  56.5 0.6 copy-done.20
  57.1 5.1 %all-gather.1 = bf16[4,2,256]{2,1,0:T(2,128)(2,1)S(1)} all-gather(bf16[1,2,256]{2,1,0:T(2,128)(2,1)S(1)} %bitcast.139), channel_id=1, replica_groups=mesh['frame'=4,'cam'=8] {'frame'}, dimensions={0}, use_global_device_ids=true | all-gather | bytes 5120 | tf_op jit(solution)/shard_map/all_gather | solution.py:77
  62.2 149.6 %reduce-scatter.4.cloned.1.call-done = f32[2048,2]{1,0:T(8,128)} async-done(((f32[16384,2]{1,0:T(8,128)}), f32[2048,2]{1,0:T(8,128)}) %reduce-scatter.4.cloned.1.call-update) | async-done | bytes 16400
  211.8 1.6 copy.15
  213.5 5.2 %all-gather = bf16[4,2,2048]{2,1,0:T(2,128)(2,1)S(1)} all-gather(bf16[1,2,2048]{2,1,0:T(2,128)(2,1)S(1)} %fusion.69), channel_id=1, replica_groups=mesh['frame'=4,'cam'=8] {'frame'}, dimensions={0}, use_global_device_ids=true | all-gather | bytes 40960 | tf_op jit(solution)/shard_map/all_gather | solution.py:76
  219.0 20.2 %psum.14 = f32[2,256]{1,0:T(2,128)} all-reduce(f32[2,256]{1,0:T(2,128)S(1)} %fusion.35), channel_id=1, replica_groups=mesh['frame'=4,'cam'=8] {'cam'}, use_global_device_ids=true, to_apply=%region_2.3 | all-reduce | flops 512 | bytes 4096 | tf_op jit(solution)/shard_map/psum | solution.py:54
  239.2 1.1 fusion.28
  240.3 40.5 %all-reduce.3.cloned.1.call-done = f32[9,256,256]{2,1,0:T(8,128)} async-done(((f32[9,256,256]{2,1,0:T(8,128)}), f32[9,256,256]{2,1,0:T(8,128)}) %all-reduce.3.cloned.1.call-update) | async-done | bytes 2359312 | tf_op jit(solution)/shard_map/psum | solution.py:83
  280.7 3.2 %copy.36 = f32[9,256,256]{2,1,0:T(8,128)} copy(f32[9,256,256]{2,1,0:T(8,128)} %all-reduce.3.cloned.1.call-done) | data formatting | bytes 4718592
  (58 shorter events, 2.1 us)
Async XLA Ops:
  8.0 1.2 copy-start
  8.0 9.1 %copy-start.1 = (bf16[2,11,2,32,256]{4,3,2,1,0:T(8,128)(2,1)S(1)}, bf16[2,11,2,32,256]{4,3,2,1,0:T(8,128)(2,1)}, u32[]{:S(2)}) copy-start(bf16[2,11,2,32,256]{4,3,2,1,0:T(8,128)(2,1)} %param.5) | copy-start | bytes 2162692
  8.0 203.8 %reduce-scatter.4.cloned.1.call-start = ((), (), s32[]{:S(2)}) async-start(), calls=%async_computation.2 | async-start | bytes 9437184
  10.3 18.7 %collective-permute-start = (bf16[2,2048]{1,0:T(2,128)(2,1)S(1)}, bf16[2,2048]{1,0:T(2,128)(2,1)S(1)}, u32[]{:S(2)}, u32[]{:S(2)}) collective-permute-start(bf16[2,2048]{1,0:T(2,128)(2,1)S(1)} %get-tuple-element.14), channel_id=1, source_target_pairs={{0,7},{1,0},{2,1},{3,2},{4,3},{5,4},{6,5},{7,6},{8,15},{9,8},{10,9... | collective-permute-start | bytes 24584 | tf_op jit(solution)/shard_map/ppermute | solution.py:12
  17.1 2.5 copy-start.21
  19.6 7.4 %copy-start.5 = (bf16[2,11,2,32,256]{4,3,2,1,0:T(8,128)(2,1)}, bf16[2,11,2,32,256]{4,3,2,1,0:T(8,128)(2,1)S(1)}, u32[]{:S(2)}) copy-start(bf16[2,11,2,32,256]{4,3,2,1,0:T(8,128)(2,1)S(1)} %get-tuple-element.11) | copy-start | bytes 2162692
  19.6 7.8 %copy-start.3 = (bf16[2,11,2,32,256]{4,3,2,1,0:T(8,128)(2,1)}, bf16[2,11,2,32,256]{4,3,2,1,0:T(8,128)(2,1)S(1)}, u32[]{:S(2)}) copy-start(bf16[2,11,2,32,256]{4,3,2,1,0:T(8,128)(2,1)S(1)} %get-tuple-element.5) | copy-start | bytes 2162692
  19.6 2.1 copy-start.15
  19.6 2.3 copy-start.19
  21.9 1.1 copy-start.13
  23.0 1.1 copy-start.11
  24.4 1.1 copy-start.9
  25.6 1.1 copy-start.7
  29.0 3.8 %collective-permute-start.1 = (bf16[2,4096]{1,0:T(2,128)(2,1)S(1)}, bf16[2,4096]{1,0:T(2,128)(2,1)S(1)}, u32[]{:S(2)}, u32[]{:S(2)}) collective-permute-start(bf16[2,4096]{1,0:T(2,128)(2,1)S(1)} %pad_maximum_fusion.1), channel_id=1, source_target_pairs={{0,6},{1,7},{2,0},{3,1},{4,2},{5,3},{6,4},{7,5},{8,14},{9,15},{10,... | collective-permute-start | bytes 49160 | tf_op jit(solution)/shard_map/ppermute | solution.py:12
  32.8 4.9 %collective-permute-start.2 = (bf16[2,8192]{1,0:T(2,128)(2,1)S(1)}, bf16[2,8192]{1,0:T(2,128)(2,1)S(1)}, u32[]{:S(2)}, u32[]{:S(2)}) collective-permute-start(bf16[2,8192]{1,0:T(2,128)(2,1)S(1)} %pad_maximum_fusion), channel_id=1, source_target_pairs={{0,4},{1,5},{2,6},{3,7},{4,0},{5,1},{6,2},{7,3},{8,12},{9,13},{10,... | collective-permute-start | bytes 98312 | tf_op jit(solution)/shard_map/ppermute | solution.py:12
  39.5 2.5 copy-start.17
  42.0 1.1 copy-start.16
  42.0 1.5 copy-start.14
  43.1 1.2 copy-start.12
  43.5 1.2 copy-start.2
  44.3 1.2 copy-start.10
  44.7 1.2 copy-start.8
  45.4 1.2 copy-start.6
  47.0 1.4 copy-start.18
  54.3 1.1 copy-start.4
  54.3 226.5 %all-reduce.3.cloned.1.call-start = ((), (), s32[]{:S(2)}) async-start(), calls=%async_computation.1 | async-start | bytes 4718592 | tf_op jit(solution)/shard_map/psum | solution.py:83
  56.5 0.7 copy-start.20
Sparse Core Ops, SparseCore 0:
  54.4 157.3 reduce-scatter.3
Sparse Core Ops, SparseCore 1:
  60.9 219.8 all-reduce.2
